TPU v7x, 32 devices: a whole 2x2x4 slice. The times are simulated.
32 devices in a mesh: groups: 2 (over y), row: 4 (over x, core), col: 4 (over z).
Axes of the slice: x: 2, y: 2, z: 4, core: 2. Of those that a mesh axis runs over, the one named last changes fastest.
Arguments:
- right_sides: float32 [32, 16384], P(None, ('groups', 'row')), parts along dimension 1
- nugget: float32 [16384], P(('groups', 'row')), parts along dimension 0, may hold values from 1 to 4
- cov_blocks: bfloat16 [8, 4, 32, 256, 256], P(('groups', 'row'), 'col'), parts along dimension 0
- block_rows: int32 [8, 4, 32], P(('groups', 'row'), 'col'), parts along dimension 0, may hold values from 0 to 7, as said below
- block_cols: int32 [8, 4, 32], P(('groups', 'row'), 'col'), parts along dimension 0, may hold values from 0 to 7, as said below
- block_count: int32 [8, 4], P(('groups', 'row'), 'col'), parts along dimension 0, may hold values from 4 to 32, as said below
Outputs:
- solution: float32 [32, 16384], P(None, ('groups', 'row')), parts along dimension 1
- residual: float32 [32, 16384], P(None, ('groups', 'row')), parts along dimension 1
There are 2 independent parts, one for each index of `groups`. A program takes and returns all parts, laid end to end along the dimension named above; each array names one. Nothing has to cross between parts.
Inputs may be any that keep to these rules, and one draw needn't show every extreme that they name: On each device the pairs (block_rows, block_cols) of all 32 slots are distinct; no stored block position of a problem is the mirror image of another (no pair is stored both as (g, h) and as (h, g)); on devices whose row and col index are equal, block_rows <= block_cols. `block_cols`: see block_rows. `block_count`: slots at or beyond the count are empty; some device of every problem has exactly 32 live slots.
All inputs are finite; a program needn't handle non-finite values.
Results may differ from a plain program's by a relative error of at most 0.0003.
Values sent between devices are 32-bit elements; how exact they have to be, the bound alone decides.
A program may use at most 64 MiB of HBM per device.

v0:
```python
import jax
import jax.numpy as jnp
from jax import lax
from jax.sharding import PartitionSpec as P

ITERS = 2


def from_root(value, axis, source):
    kept = jnp.where(lax.axis_index(axis) == source, value, 0).astype(value.dtype)
    return lax.psum(kept, axis)


def on_device(right_sides, nugget, cov_blocks, block_rows, block_cols, block_count):
    blocks = cov_blocks[0, 0].astype(jnp.float32)
    slot_rows = block_rows[0, 0]
    slot_cols = block_cols[0, 0]
    live_count = block_count[0, 0]
    slot_total = blocks.shape[0]
    tile_size = blocks.shape[1]
    series, row_width = right_sides.shape
    tile_count = row_width // tile_size
    live_mask = (jnp.arange(slot_total, dtype=jnp.int32) < live_count).astype(jnp.float32)
    block_ids = jnp.arange(tile_count, dtype=jnp.int32)[:, None]
    row_selector = (slot_rows[None, :] == block_ids).astype(jnp.float32) * live_mask[None, :]
    col_selector = (slot_cols[None, :] == block_ids).astype(jnp.float32) * live_mask[None, :]

    def spread(selector, values):
        placed = jnp.einsum("bm,rmj->rbj", selector, values, precision=lax.Precision.HIGHEST)
        return placed.reshape(series, row_width)

    solution = jnp.zeros_like(right_sides)
    residual = right_sides
    direction = right_sides
    norm_now = lax.psum(jnp.sum(residual * residual, axis=1), "row")
    for turn_index in range(ITERS):
        far_rows = from_root(direction, "row", lax.axis_index("col"))
        near_tiles = direction.reshape(series, tile_count, tile_size)
        far_tiles = far_rows.reshape(series, tile_count, tile_size)
        local_direct = jnp.einsum(
            "rmk,mjk->rmj",
            jnp.take(far_tiles, slot_cols, axis=1),
            blocks,
            precision=lax.Precision.HIGHEST,
        )
        local_mirror = jnp.einsum(
            "rmj,mjk->rmk",
            jnp.take(near_tiles, slot_rows, axis=1),
            blocks,
            precision=lax.Precision.HIGHEST,
        )
        apply_direct = spread(row_selector, local_direct)
        apply_mirror = spread(col_selector, local_mirror)
        total = lax.psum(apply_direct, "col")
        summed = lax.psum(apply_mirror, "row")
        total = total + from_root(summed, "col", lax.axis_index("row"))
        applied = nugget[None, :] * direction + total
        curvature, crossed, squared = lax.psum(
            (
                jnp.sum(direction * applied, axis=1),
                jnp.sum(residual * applied, axis=1),
                jnp.sum(applied * applied, axis=1),
            ),
            "row",
        )
        step_size = norm_now / curvature
        solution = solution + step_size[:, None] * direction
        residual = residual - step_size[:, None] * applied
        norm_next = norm_now - 2.0 * step_size * crossed + step_size * step_size * squared
        direction = residual + (norm_next / norm_now)[:, None] * direction
        norm_now = norm_next
    return (solution, residual)


def solution(mesh):
    placed = (
        P(None, ("groups", "row")),
        P(("groups", "row")),
        P(("groups", "row"), "col", None, None, None),
        P(("groups", "row"), "col", None),
        P(("groups", "row"), "col", None),
        P(("groups", "row"), "col"),
    )
    return jax.shard_map(
        on_device,
        mesh=mesh,
        in_specs=placed,
        out_specs=(P(None, ("groups", "row")), P(None, ("groups", "row"))),
        check_vma=False,
    )
```

profile of v0, /device:TPU:0, one launch (start us, length us, event | category | flops | bytes accessed | tf_op | source)
XLA Modules:
  0.0 210.6 jit_solution(2557300919919235164)
XLA Ops:
  9.2 1.0 copy.38
  10.2 1.0 broadcast_select_fusion.1
  12.5 4.4 %fusion.11 = f32[32,32,256]{2,0,1:T(8,128)S(1)} fusion(bf16[1,1,32,256,256]{4,3,2,1,0:T(8,128)(2,1)} %param.10, f32[32,32,256]{2,1,0:T(8,128)S(1)} %gather_fusion.1, pred[32]{0:T(512)(128)(4,1)S(1)} %compare_and_fusion), kind=kOutput, calls=%fused_computation.13 | convolution fusion | flops 805568512 | bytes 6291488 | tf_op jit(solution)/shard_map/rmj,mjk->rmk/dot_general | solution.py:46
  16.9 1.2 fusion.28
  18.2 0.8 copy.21
  19.1 35.7 %all-reduce.14.cloned.1.call-done = (f32[32,8,256]{2,0,1:T(8,128)}, f32[32,2048]{1,0:T(8,128)}) async-done(((f32[32,8,256]{2,0,1:T(8,128)}, f32[32,2048]{1,0:T(8,128)}), (f32[32,8,256]{2,0,1:T(8,128)}, f32[32,2048]{1,0:T(8,128)})) %all-reduce.14.cloned.1.call-update) | async-done | bytes 524304 | tf_op jit(solution)/shard_map/psum | solution.py:11
  54.8 1.6 gather_fusion
  56.4 6.0 %fusion.8 = f32[32,32,256]{2,0,1:T(8,128)S(1)} fusion(bf16[1,1,32,256,256]{4,3,2,1,0:T(8,128)(2,1)} %param.10, f32[32,32,256]{2,1,0:T(8,128)S(1)} %gather_fusion, pred[32]{0:T(512)(128)(4,1)S(1)} %compare_and_fusion.1), kind=kOutput, calls=%fused_computation.12 | convolution fusion | flops 805568512 | bytes 6291488 | tf_op jit(solution)/shard_map/rmk,mjk->rmj/dot_general | solution.py:40
  62.4 1.2 fusion.30
  64.6 35.8 %all-reduce.8.cloned.1.call-done = f32[32,2048]{1,0:T(8,128)} async-done(((f32[32,2048]{1,0:T(8,128)}), f32[32,2048]{1,0:T(8,128)}) %all-reduce.8.cloned.1.call-update) | async-done | bytes 262160 | tf_op jit(solution)/shard_map/psum | solution.py:54
  100.4 1.2 multiply_reduce_fusion.2
  101.6 5.7 %all-reduce = (f32[32]{0:T(128)S(1)}, f32[32]{0:T(128)S(1)}, f32[32]{0:T(128)S(1)}) all-reduce(f32[32]{0:T(128)S(1)} %get-tuple-element.4, f32[32]{0:T(128)S(1)} %get-tuple-element.5, f32[32]{0:T(128)S(1)} %get-tuple-element.3), channel_id=1, replica_groups=mesh['groups'=2,'row'=4,'col'=4] {'row'}, use_global_device_ids=true, to_apply=%region_9.11 | all-reduce | flops 96 | bytes 768 | tf_op jit(solution)/shard_map/psum | solution.py:58
  107.3 1.1 broadcast_select_fusion
  109.7 4.4 %fusion.17 = f32[32,32,256]{2,0,1:T(8,128)S(1)} fusion(bf16[1,1,32,256,256]{4,3,2,1,0:T(8,128)(2,1)} %param.10, f32[32,32,256]{2,1,0:T(8,128)S(1)} %gather_fusion.3, pred[32]{0:T(512)(128)(4,1)S(1)} %compare_and_fusion), kind=kOutput, calls=%fused_computation.15 | convolution fusion | flops 805568512 | bytes 6291488 | tf_op jit(solution)/shard_map/rmj,mjk->rmk/dot_general | solution.py:46
  114.1 1.2 fusion.24
  115.3 0.8 copy.23
  116.4 33.5 %all-reduce.12.cloned.1.call-done = (f32[32,8,256]{2,0,1:T(8,128)}, f32[32,2048]{1,0:T(8,128)}) async-done(((f32[32,8,256]{2,0,1:T(8,128)}, f32[32,2048]{1,0:T(8,128)}), (f32[32,8,256]{2,0,1:T(8,128)}, f32[32,2048]{1,0:T(8,128)})) %all-reduce.12.cloned.1.call-update) | async-done | bytes 524304 | tf_op jit(solution)/shard_map/psum | solution.py:11
  149.9 1.6 gather_fusion.2
  151.5 6.0 %fusion.14 = f32[32,32,256]{2,0,1:T(8,128)S(1)} fusion(bf16[1,1,32,256,256]{4,3,2,1,0:T(8,128)(2,1)} %param.10, f32[32,32,256]{2,1,0:T(8,128)S(1)} %gather_fusion.2, pred[32]{0:T(512)(128)(4,1)S(1)} %compare_and_fusion.1), kind=kOutput, calls=%fused_computation.14 | convolution fusion | flops 805568512 | bytes 6291488 | tf_op jit(solution)/shard_map/rmk,mjk->rmj/dot_general | solution.py:40
  157.5 1.2 fusion.26
  159.6 35.9 %all-reduce.10.cloned.1.call-done = f32[32,2048]{1,0:T(8,128)} async-done(((f32[32,2048]{1,0:T(8,128)}), f32[32,2048]{1,0:T(8,128)}) %all-reduce.10.cloned.1.call-update) | async-done | bytes 262160 | tf_op jit(solution)/shard_map/psum | solution.py:54
  195.4 1.1 multiply_reduce_fusion
  196.5 5.7 %psum.98 = f32[32]{0:T(128)S(1)} all-reduce(f32[32]{0:T(128)S(1)} %multiply_reduce_fusion), channel_id=1, replica_groups=mesh['groups'=2,'row'=4,'col'=4] {'row'}, use_global_device_ids=true, to_apply=%region_15.17 | all-reduce | flops 32 | bytes 256 | tf_op jit(solution)/shard_map/psum | solution.py:58
  202.2 1.9 multiply_subtract_fusion
  (40 shorter events, 6.2 us)
Async XLA Ops:
  7.2 47.6 %all-reduce.14.cloned.1.call-start = ((), (), s32[]{:S(2)}) async-start(), calls=%async_computation.3 | async-start | bytes 1048576 | tf_op jit(solution)/shard_map/psum | solution.py:11
  11.9 5.0 %copy-start.5 = (s32[1,1,32]{2,1,0:T(1,128)S(1)}, s32[1,1,32]{2,1,0:T(1,128)}, u32[]{:S(2)}) copy-start(s32[1,1,32]{2,1,0:T(1,128)} %param.12) | copy-start | bytes 388
  19.0 81.4 %all-reduce.8.cloned.1.call-start = ((), (), s32[]{:S(2)}) async-start(), calls=%async_computation | async-start | bytes 524288 | tf_op jit(solution)/shard_map/psum | solution.py:54
  54.8 7.6 %copy-start.6 = (s32[1,1,32]{2,1,0:T(1,128)S(1)}, s32[1,1,32]{2,1,0:T(1,128)}, u32[]{:S(2)}) copy-start(s32[1,1,32]{2,1,0:T(1,128)} %param.11) | copy-start | bytes 388
  56.4 7.4 %copy-start.2 = (f32[32,2048]{1,0:T(8,128)S(1)}, f32[32,2048]{1,0:T(8,128)}, u32[]{:S(2)}) copy-start(f32[32,2048]{1,0:T(8,128)} %get-tuple-element.12) | copy-start | bytes 786436
  56.4 44.0 %copy-start = (f32[32,2048]{1,0:T(8,128)S(1)}, f32[32,2048]{1,0:T(8,128)}, u32[]{:S(2)}) copy-start(f32[32,2048]{1,0:T(8,128)} %param.8) | copy-start | bytes 786436
  56.4 44.0 %copy-start.4 = (f32[2048]{0:T(1024)S(1)}, f32[2048]{0:T(1024)}, u32[]{:S(2)}) copy-start(f32[2048]{0:T(1024)} %param.9) | copy-start | bytes 24580
  64.5 85.4 %all-reduce.12.cloned.1.call-start = ((), (), s32[]{:S(2)}) async-start(), calls=%async_computation.2 | async-start | bytes 1048576 | tf_op jit(solution)/shard_map/psum | solution.py:11
  116.1 79.3 %all-reduce.10.cloned.1.call-start = ((), (), s32[]{:S(2)}) async-start(), calls=%async_computation.1 | async-start | bytes 524288 | tf_op jit(solution)/shard_map/psum | solution.py:54
  151.5 7.4 %copy-start.3 = (f32[32,2048]{1,0:T(8,128)S(1)}, f32[32,2048]{1,0:T(8,128)}, u32[]{:S(2)}) copy-start(f32[32,2048]{1,0:T(8,128)} %get-tuple-element.10) | copy-start | bytes 786436
  151.5 50.7 %copy-start.1 = (f32[32,2048]{1,0:T(8,128)S(1)}, f32[32,2048]{1,0:T(8,128)}, u32[]{:S(2)}) copy-start(f32[32,2048]{1,0:T(8,128)} %all-reduce.8.cloned.1.call-done) | copy-start | bytes 786436
Sparse Core Ops, SparseCore 0:
  19.1 35.6 all-reduce.13
  64.6 35.7 all-reduce.7
  116.3 33.5 all-reduce.11
  159.7 35.6 all-reduce.9
where the time goes:
time: 211 us
  waiting for transfers between devices  141 us (67%)
  matrix products  25.7 us (12%)
  between operations  14.7 us (7%)
  blocking collectives  11.3 us (5%)
  other arithmetic  9.03 us (4%)
  local copies, waits for them, and re-layouts  8.58 us (4%)
    psum x2, waiting for transfers between devices, on_device(): total = lax.psum(apply_direct, 'col')  71.7 us
    psum x2, waiting for transfers between devices, from_root(): return lax.psum(kept, axis)  69.2 us
    dot_general x2, matrix products, on_device(): jnp.einsum('rmk,mjk->rmj', jnp.take(far_tiles, slot_cols, axis=1), blocks...  12 us
    psum x2, blocking collectives, on_device(): lax.psum((jnp.sum(direction * applied, axis=1), jnp.sum(residual * applie...  11.3 us
    dot_general x2, matrix products, on_device(): jnp.einsum('rmj,mjk->rmk', jnp.take(near_tiles, slot_rows, axis=1), block...  8.74 us
    dot_general x4, matrix products, spread(): jnp.einsum('bm,rmj->rbj', selector, values, precision=lax.Precision.HIGHEST)  4.95 us
  transfers between devices with their start and end apart: 4, of which 4 were waited for; matrix products, arithmetic and copies ran while one was open for 0% of the time, Pallas kernels for 0%

commit v1 on v0

--- a/solution.py
+++ b/solution.py
@@ -51,7 +51,9 @@
         )
         apply_direct = spread(row_selector, local_direct)
         apply_mirror = spread(col_selector, local_mirror)
-        total = lax.psum(apply_direct, "col")
+        total = apply_direct
+        for hop in (1, 2):
+            total = total + lax.ppermute(total, "col", [(dev, dev ^ hop) for dev in range(4)])
         summed = lax.psum(apply_mirror, "row")
         total = total + from_root(summed, "col", lax.axis_index("row"))
         applied = nugget[None, :] * direction + total

time: 211 us -> 226 us (1.071)
  starting transfers between devices: 0.35 us -> 8.89 us
  waiting for transfers between devices: 141 us -> 148 us
    ppermute x0 -> x4, waiting for transfers between devices: none -> 9.22 us  [on_device(): lax.ppermute(total, 'col', [(dev, dev ^ hop) for dev in range(4)])]
    ppermute x0 -> x4, starting transfers between devices: none -> 8.55 us  [on_device(): lax.ppermute(total, 'col', [(dev, dev ^ hop) for dev in range(4)])]
    psum x2, waiting for transfers between devices: 71.7 us -> 69.3 us  [on_device(): summed = lax.psum(apply_mirror, 'row')]
  transfers between devices with their start and end apart: 4 -> 8, of which waited for: 4 -> 6; matrix products, arithmetic and copies ran while one was open for 0% -> 1% of each run, Pallas kernels for 0% -> 0%
where the time goes in v1:
time: 226 us; the launch traced here: 225 us
  waiting for transfers between devices  148 us (65%)
  matrix products  25.6 us (11%)
  between operations  14.7 us (7%)
  blocking collectives  11.3 us (5%)
  starting transfers between devices  8.89 us (4%)
  local copies, waits for them, and re-layouts  8.58 us (4%)
  other arithmetic  8.14 us (4%)
    psum x2, waiting for transfers between devices, from_root(): return lax.psum(kept, axis)  69.3 us
    psum x2, waiting for transfers between devices, on_device(): summed = lax.psum(apply_mirror, 'row')  69.3 us
    dot_general x2, matrix products, on_device(): jnp.einsum('rmk,mjk->rmj', jnp.take(far_tiles, slot_cols, axis=1), blocks...  12 us
    psum x2, blocking collectives, on_device(): lax.psum((jnp.sum(direction * applied, axis=1), jnp.sum(residual * applie...  11.3 us
    ppermute x4, waiting for transfers between devices, on_device(): lax.ppermute(total, 'col', [(dev, dev ^ hop) for dev in range(4)])  9.22 us
    dot_general x2, matrix products, on_device(): jnp.einsum('rmj,mjk->rmk', jnp.take(near_tiles, slot_rows, axis=1), block...  8.74 us
    ppermute x4, starting transfers between devices, on_device(): lax.ppermute(total, 'col', [(dev, dev ^ hop) for dev in range(4)])  8.55 us
    dot_general x4, matrix products, spread(): jnp.einsum('bm,rmj->rbj', selector, values, precision=lax.Precision.HIGHEST)  4.95 us
  transfers between devices with their start and end apart: 8, of which 6 were waited for; matrix products, arithmetic and copies ran while one was open for 1% of the time, Pallas kernels for 0%

profile of v1, /device:TPU:0, one launch (start us, length us, event | category | flops | bytes accessed | tf_op | source)
XLA Modules:
  0.0 225.1 jit_solution(2256271047653826565)
XLA Ops:
  12.5 4.4 %fusion.11 = f32[32,32,256]{2,0,1:T(8,128)S(1)} fusion(bf16[1,1,32,256,256]{4,3,2,1,0:T(8,128)(2,1)} %param.10, f32[32,32,256]{2,1,0:T(8,128)S(1)} %gather_fusion.1, pred[32]{0:T(512)(128)(4,1)S(1)} %compare_and_fusion), kind=kOutput, calls=%fused_computation.13 | convolution fusion | flops 805568512 | bytes 6291488 | tf_op jit(solution)/shard_map/rmj,mjk->rmk/dot_general | solution.py:46
  16.9 1.2 fusion.28
  19.1 35.7 %all-reduce.14.cloned.1.call-done = (f32[32,2048]{1,0:T(8,128)}, f32[32,8,256]{2,0,1:T(8,128)}) async-done(((f32[32,2048]{1,0:T(8,128)}, f32[32,8,256]{2,0,1:T(8,128)}), (f32[32,2048]{1,0:T(8,128)}, f32[32,8,256]{2,0,1:T(8,128)})) %all-reduce.14.cloned.1.call-update) | async-done | bytes 524304 | tf_op jit(solution)/shard_map/psum | solution.py:57
  54.8 1.6 gather_fusion
  56.4 6.0 %fusion.8 = f32[32,32,256]{2,0,1:T(8,128)S(1)} fusion(bf16[1,1,32,256,256]{4,3,2,1,0:T(8,128)(2,1)} %param.10, f32[32,32,256]{2,1,0:T(8,128)S(1)} %gather_fusion, pred[32]{0:T(512)(128)(4,1)S(1)} %compare_and_fusion.1), kind=kOutput, calls=%fused_computation.12 | convolution fusion | flops 805568512 | bytes 6291488 | tf_op jit(solution)/shard_map/rmk,mjk->rmj/dot_general | solution.py:40
  62.4 1.2 fusion.30
  63.7 1.6 collective-permute-start
  66.1 4.6 %collective-permute-done = f32[32,2048]{1,0:T(8,128)S(1)} collective-permute-done((f32[32,2048]{1,0:T(8,128)S(1)}, f32[32,2048]{1,0:T(8,128)S(1)}, u32[]{:S(2)}, u32[]{:S(2)}) %collective-permute-start) | collective-permute-done | bytes 262176 | tf_op jit(solution)/shard_map/ppermute | solution.py:56
  70.7 2.7 %collective-permute-start.1 = (f32[32,2048]{1,0:T(8,128)S(1)}, f32[32,2048]{1,0:T(8,128)S(1)}, u32[]{:S(2)}, u32[]{:S(2)}) collective-permute-start(f32[32,2048]{1,0:T(8,128)S(1)} %add.60), channel_id=1, source_target_pairs={{0,2},{1,3},{2,0},{3,1},{4,6},{5,7},{6,4},{7,5},{8,10},{9,11},{10,... | collective-permute-start | bytes 786440 | tf_op jit(solution)/shard_map/ppermute | solution.py:56
  73.4 34.6 %all-reduce.8.cloned.1.call-done = f32[32,2048]{1,0:T(8,128)} async-done(((f32[32,2048]{1,0:T(8,128)}), f32[32,2048]{1,0:T(8,128)}) %all-reduce.8.cloned.1.call-update) | async-done | bytes 262160 | tf_op jit(solution)/shard_map/psum | solution.py:11
  108.1 1.2 multiply_reduce_fusion.2
  109.3 5.7 %all-reduce = (f32[32]{0:T(128)S(1)}, f32[32]{0:T(128)S(1)}, f32[32]{0:T(128)S(1)}) all-reduce(f32[32]{0:T(128)S(1)} %get-tuple-element.4, f32[32]{0:T(128)S(1)} %get-tuple-element.5, f32[32]{0:T(128)S(1)} %get-tuple-element.3), channel_id=1, replica_groups=mesh['groups'=2,'row'=4,'col'=4] {'row'}, use_global_device_ids=true, to_apply=%region_8.10 | all-reduce | flops 96 | bytes 768 | tf_op jit(solution)/shard_map/psum | solution.py:60
  116.4 4.4 %fusion.17 = f32[32,32,256]{2,0,1:T(8,128)S(1)} fusion(bf16[1,1,32,256,256]{4,3,2,1,0:T(8,128)(2,1)} %param.10, f32[32,32,256]{2,1,0:T(8,128)S(1)} %gather_fusion.3, pred[32]{0:T(512)(128)(4,1)S(1)} %compare_and_fusion), kind=kOutput, calls=%fused_computation.15 | convolution fusion | flops 805568512 | bytes 6291488 | tf_op jit(solution)/shard_map/rmj,mjk->rmk/dot_general | solution.py:46
  120.8 1.2 fusion.24
  123.1 33.5 %all-reduce.12.cloned.1.call-done = (f32[32,2048]{1,0:T(8,128)}, f32[32,8,256]{2,0,1:T(8,128)}) async-done(((f32[32,2048]{1,0:T(8,128)}, f32[32,8,256]{2,0,1:T(8,128)}), (f32[32,2048]{1,0:T(8,128)}, f32[32,8,256]{2,0,1:T(8,128)})) %all-reduce.12.cloned.1.call-update) | async-done | bytes 524304 | tf_op jit(solution)/shard_map/psum | solution.py:57
  156.6 1.6 gather_fusion.2
  158.2 6.0 %fusion.14 = f32[32,32,256]{2,0,1:T(8,128)S(1)} fusion(bf16[1,1,32,256,256]{4,3,2,1,0:T(8,128)(2,1)} %param.10, f32[32,32,256]{2,1,0:T(8,128)S(1)} %gather_fusion.2, pred[32]{0:T(512)(128)(4,1)S(1)} %compare_and_fusion.1), kind=kOutput, calls=%fused_computation.14 | convolution fusion | flops 805568512 | bytes 6291488 | tf_op jit(solution)/shard_map/rmk,mjk->rmj/dot_general | solution.py:40
  164.2 1.2 fusion.26
  165.5 1.6 collective-permute-start.2
  167.8 4.6 %collective-permute-done.2 = f32[32,2048]{1,0:T(8,128)S(1)} collective-permute-done((f32[32,2048]{1,0:T(8,128)S(1)}, f32[32,2048]{1,0:T(8,128)S(1)}, u32[]{:S(2)}, u32[]{:S(2)}) %collective-permute-start.2) | collective-permute-done | bytes 262176 | tf_op jit(solution)/shard_map/ppermute | solution.py:56
  172.5 2.7 %collective-permute-start.3 = (f32[32,2048]{1,0:T(8,128)S(1)}, f32[32,2048]{1,0:T(8,128)S(1)}, u32[]{:S(2)}, u32[]{:S(2)}) collective-permute-start(f32[32,2048]{1,0:T(8,128)S(1)} %add.66), channel_id=1, source_target_pairs={{0,2},{1,3},{2,0},{3,1},{4,6},{5,7},{6,4},{7,5},{8,10},{9,11},{10,... | collective-permute-start | bytes 786440 | tf_op jit(solution)/shard_map/ppermute | solution.py:56
  175.2 34.6 %all-reduce.10.cloned.1.call-done = f32[32,2048]{1,0:T(8,128)} async-done(((f32[32,2048]{1,0:T(8,128)}), f32[32,2048]{1,0:T(8,128)}) %all-reduce.10.cloned.1.call-update) | async-done | bytes 262160 | tf_op jit(solution)/shard_map/psum | solution.py:11
  211.0 5.7 %psum.82 = f32[32]{0:T(128)S(1)} all-reduce(f32[32]{0:T(128)S(1)} %multiply_reduce_fusion), channel_id=1, replica_groups=mesh['groups'=2,'row'=4,'col'=4] {'row'}, use_global_device_ids=true, to_apply=%region_13.15 | all-reduce | flops 32 | bytes 256 | tf_op jit(solution)/shard_map/psum | solution.py:60
  216.7 1.9 multiply_subtract_fusion
  (48 shorter events, 10.9 us)
Async XLA Ops:
  7.2 47.6 %all-reduce.14.cloned.1.call-start = ((), (), s32[]{:S(2)}) async-start(), calls=%async_computation.3 | async-start | bytes 1048576 | tf_op jit(solution)/shard_map/psum | solution.py:57
  11.9 5.0 %copy-start.4 = (s32[1,1,32]{2,1,0:T(1,128)S(1)}, s32[1,1,32]{2,1,0:T(1,128)}, u32[]{:S(2)}) copy-start(s32[1,1,32]{2,1,0:T(1,128)} %param.12) | copy-start | bytes 388
  19.0 89.1 %all-reduce.8.cloned.1.call-start = ((), (), s32[]{:S(2)}) async-start(), calls=%async_computation | async-start | bytes 524288 | tf_op jit(solution)/shard_map/psum | solution.py:11
  54.8 7.6 %copy-start.5 = (s32[1,1,32]{2,1,0:T(1,128)S(1)}, s32[1,1,32]{2,1,0:T(1,128)}, u32[]{:S(2)}) copy-start(s32[1,1,32]{2,1,0:T(1,128)} %param.11) | copy-start | bytes 388
  56.4 8.9 %copy-start.1 = (f32[32,2048]{1,0:T(8,128)S(1)}, f32[32,2048]{1,0:T(8,128)}, u32[]{:S(2)}) copy-start(f32[32,2048]{1,0:T(8,128)} %get-tuple-element.11) | copy-start | bytes 786436
  56.4 51.7 %copy-start = (f32[32,2048]{1,0:T(8,128)S(1)}, f32[32,2048]{1,0:T(8,128)}, u32[]{:S(2)}) copy-start(f32[32,2048]{1,0:T(8,128)} %param.8) | copy-start | bytes 786436
  56.4 51.7 %copy-start.3 = (f32[2048]{0:T(1024)S(1)}, f32[2048]{0:T(1024)}, u32[]{:S(2)}) copy-start(f32[2048]{0:T(1024)} %param.9) | copy-start | bytes 24580
  63.7 6.9 %collective-permute-start = (f32[32,2048]{1,0:T(8,128)S(1)}, f32[32,2048]{1,0:T(8,128)S(1)}, u32[]{:S(2)}, u32[]{:S(2)}) collective-permute-start(f32[32,2048]{1,0:T(8,128)S(1)} %bitcast.89), channel_id=1, source_target_pairs={{0,1},{1,0},{2,3},{3,2},{4,5},{5,4},{6,7},{7,6},{8,9},{9,8},{10,11... | collective-permute-start | bytes 786440 | tf_op jit(solution)/shard_map/ppermute | solution.py:56
  66.0 90.6 %all-reduce.12.cloned.1.call-start = ((), (), s32[]{:S(2)}) async-start(), calls=%async_computation.2 | async-start | bytes 1048576 | tf_op jit(solution)/shard_map/psum | solution.py:57
  70.7 37.4 %collective-permute-start.1 = (f32[32,2048]{1,0:T(8,128)S(1)}, f32[32,2048]{1,0:T(8,128)S(1)}, u32[]{:S(2)}, u32[]{:S(2)}) collective-permute-start(f32[32,2048]{1,0:T(8,128)S(1)} %add.60), channel_id=1, source_target_pairs={{0,2},{1,3},{2,0},{3,1},{4,6},{5,7},{6,4},{7,5},{8,10},{9,11},{10,... | collective-permute-start | bytes 786440 | tf_op jit(solution)/shard_map/ppermute | solution.py:56
  122.9 87.0 %all-reduce.10.cloned.1.call-start = ((), (), s32[]{:S(2)}) async-start(), calls=%async_computation.1 | async-start | bytes 524288 | tf_op jit(solution)/shard_map/psum | solution.py:11
  158.2 8.9 %copy-start.2 = (f32[32,2048]{1,0:T(8,128)S(1)}, f32[32,2048]{1,0:T(8,128)}, u32[]{:S(2)}) copy-start(f32[32,2048]{1,0:T(8,128)} %get-tuple-element.9) | copy-start | bytes 786436
  165.5 6.9 %collective-permute-start.2 = (f32[32,2048]{1,0:T(8,128)S(1)}, f32[32,2048]{1,0:T(8,128)S(1)}, u32[]{:S(2)}, u32[]{:S(2)}) collective-permute-start(f32[32,2048]{1,0:T(8,128)S(1)} %bitcast.91), channel_id=1, source_target_pairs={{0,1},{1,0},{2,3},{3,2},{4,5},{5,4},{6,7},{7,6},{8,9},{9,8},{10,11... | collective-permute-start | bytes 786440 | tf_op jit(solution)/shard_map/ppermute | solution.py:56
  172.5 37.4 %collective-permute-start.3 = (f32[32,2048]{1,0:T(8,128)S(1)}, f32[32,2048]{1,0:T(8,128)S(1)}, u32[]{:S(2)}, u32[]{:S(2)}) collective-permute-start(f32[32,2048]{1,0:T(8,128)S(1)} %add.66), channel_id=1, source_target_pairs={{0,2},{1,3},{2,0},{3,1},{4,6},{5,7},{6,4},{7,5},{8,10},{9,11},{10,... | collective-permute-start | bytes 786440 | tf_op jit(solution)/shard_map/ppermute | solution.py:56
Sparse Core Ops, SparseCore 0:
  19.1 35.6 all-reduce.13
  66.2 41.8 all-reduce.7
  123.0 33.5 all-reduce.11
  168.0 41.8 all-reduce.9
